TPU v7x, 512 devices: a whole 4x8x8 slice. The times are simulated.
512 devices in a mesh: gx: 32 (over y, x), gy: 16 (over z, core).
Axes of the slice: x: 4, y: 8, z: 8, core: 2. Of those that a mesh axis runs over, the one named last changes fastest.
Arguments:
- hidden_in: bfloat16 [4096, 2560], P('gx'), may hold values from -48 to 48
- norm_gain: bfloat16 [2560], replicated, may hold values from 0.099609375 to 1.8984375
- router_weight: bfloat16 [2560, 64], replicated, may hold values from -3 to 3
- routes: int32 [4096, 6], P('gx'), may hold values from 0 to 63, as said below
- w_gate_up: bfloat16 [512, 2560, 384], P(('gx', 'gy')), may hold values from -0.125 to 0.125
- w_down: bfloat16 [512, 192, 2560], P(('gx', 'gy')), may hold values from -0.15625 to 0.15625
- final_gain: bfloat16 [2560], replicated, may hold values from 0.099609375 to 1.8984375
- head_weight: bfloat16 [2560, 53248], P('gy', 'gx'), may hold values from -5 to 5
- targets: int32 [4096], replicated, may hold values from 0 to 53247
Outputs:
- logprob: float32 [32, 128], P(None, 'gy')
- entropy: float32 [32, 128], P(None, 'gy')
Inputs may be any that keep to these rules, and one draw needn't show every extreme that they name: `routes`: each row names 6 different experts. Within the 128 rows of one index of gx no expert is named by more than 16 rows, and one expert, the same for every index of gx, is named by exactly 16 rows in each.
All inputs are finite; a program needn't handle non-finite values.
Results may differ from a plain program's by a relative error of at most 0.012.
Values may be sent and summed in bfloat16 or wider, within the bound.
A program may use at most 192 MiB of HBM per device.

v0:
```python
import jax
import jax.numpy as jnp
from jax import lax
from jax.sharding import PartitionSpec as P

SPLITS = 8
NORM_EPSILON = 1e-06


def rms_scale(values, gain_vector):
    widened = values.astype(jnp.float32)
    return (
        widened
        * lax.rsqrt(jnp.mean(widened * widened, -1, keepdims=True) + NORM_EPSILON)
        * gain_vector.astype(jnp.float32)
    )


def finish(peak_value, total_mass, spread, target_logit):
    log_mass = jnp.log(total_mass)
    return (target_logit - peak_value - log_mass, log_mass - spread / total_mass)


def shards(
    hidden_in, norm_gain, router_weight, routes, w_gate_up, w_down, final_gain, head_weight, targets
):
    tok_rows = hidden_in.shape[0]
    group_count = lax.axis_size("gx")
    lane_count = lax.axis_size("gy")
    group_index = lax.axis_index("gx")
    lane_index = lax.axis_index("gy")
    expert_count = router_weight.shape[1]
    held_slices = w_gate_up.shape[0]
    unit_count = w_down.shape[1]
    slot_count = tok_rows // 8
    share_rows = tok_rows // lane_count
    columns = head_weight.shape[1]
    normed = rms_scale(hidden_in, norm_gain).astype(jnp.bfloat16)
    scores = jnp.dot(normed, router_weight, preferred_element_type=jnp.float32)
    chosen = routes[:, :, None] == jnp.arange(expert_count, dtype=jnp.int32)[None, None, :]
    picked = jnp.sum(jnp.where(chosen, scores[:, None, :], 0.0), -1)
    gate_values = jax.nn.softmax(picked, axis=-1).astype(jnp.bfloat16)
    gate_table = jnp.sum(jnp.where(chosen, gate_values.astype(jnp.float32)[:, :, None], 0.0), 1)
    member = jnp.sum(chosen.astype(jnp.int32), 1)
    slot_rank = jnp.cumsum(member, 0) - member
    slot_hit = (member[:, :, None] == 1) & (
        slot_rank[:, :, None] == jnp.arange(slot_count, dtype=jnp.int32)[None, None, :]
    )
    lane_slices = (
        jnp.arange(group_count, dtype=jnp.int32)[:, None] * lane_count + lane_index
    ) * held_slices + jnp.arange(held_slices, dtype=jnp.int32)[None, :]
    owner_expert = lane_slices // SPLITS
    pick_expert = (
        owner_expert[:, :, None] == jnp.arange(expert_count, dtype=jnp.int32)[None, None, :]
    ).astype(jnp.bfloat16)
    dispatch = jnp.einsum(
        "tke,nec->tkcn",
        pick_expert,
        slot_hit.astype(jnp.bfloat16),
        preferred_element_type=jnp.float32,
    ).astype(jnp.bfloat16)
    outgoing = jnp.einsum(
        "tkcn,nd->tkcd", dispatch, normed, preferred_element_type=jnp.float32
    ).astype(jnp.bfloat16)
    expert_gate = jnp.einsum(
        "tke,ne->tkn",
        pick_expert,
        gate_table.astype(jnp.bfloat16),
        preferred_element_type=jnp.float32,
    )
    combine = (dispatch.astype(jnp.float32) * expert_gate[:, :, None, :]).astype(jnp.bfloat16)
    lifted = jnp.einsum(
        "skcd,kdf->skcf",
        lax.all_to_all(outgoing, "gx", split_axis=0, concat_axis=0, tiled=True),
        w_gate_up,
        preferred_element_type=jnp.float32,
    )
    active = (jax.nn.silu(lifted[..., :unit_count]) * lifted[..., unit_count:]).astype(jnp.bfloat16)
    result = jnp.einsum(
        "skcf,kfd->skcd", active, w_down, preferred_element_type=jnp.float32
    ).astype(jnp.bfloat16)
    returned = lax.all_to_all(result, "gx", split_axis=0, concat_axis=0, tiled=True)
    partial_value = jnp.einsum(
        "tkcn,tkcd->nd", combine, returned, preferred_element_type=jnp.float32
    )
    summed = lax.psum_scatter(partial_value, "gy", scatter_dimension=0, tiled=True)
    residual = lax.dynamic_slice_in_dim(hidden_in, lane_index * share_rows, share_rows, 0)
    layer_out = (residual.astype(jnp.float32) + summed).astype(jnp.bfloat16)
    final_states = rms_scale(layer_out, final_gain).astype(jnp.bfloat16)
    gathered = lax.all_gather(final_states, "gx", axis=0, tiled=True)
    target_grid = targets.reshape(group_count, tok_rows)
    logits = jnp.dot(
        gathered,
        lax.all_gather(head_weight, "gy", axis=0, tiled=True),
        preferred_element_type=jnp.float32,
    )
    offset = group_index * columns
    own_targets = lax.dynamic_slice_in_dim(
        target_grid, lane_index * share_rows, share_rows, 1
    ).reshape(group_count * share_rows)
    target_hits = (offset + jnp.arange(columns, dtype=jnp.int32))[None, :] == own_targets[:, None]
    peak_value = lax.pmax(jnp.max(logits, -1), "gx")
    shifted = logits - peak_value[:, None]
    weights = jnp.exp(shifted)
    total_mass, spread, target_logit = lax.psum(
        (
            jnp.sum(weights, -1),
            jnp.sum(weights * shifted, -1),
            jnp.sum(jnp.where(target_hits, logits, 0.0), -1),
        ),
        "gx",
    )
    logprob, entropy = finish(peak_value, total_mass, spread, target_logit)
    return (logprob.reshape(group_count, share_rows), entropy.reshape(group_count, share_rows))


def solution(mesh):
    return jax.shard_map(
        shards,
        mesh=mesh,
        in_specs=(
            P("gx", None),
            P(),
            P(),
            P("gx", None),
            P(("gx", "gy"), None, None),
            P(("gx", "gy"), None, None),
            P(),
            P("gy", "gx"),
            P(),
        ),
        out_specs=(P(None, "gy"), P(None, "gy")),
        check_vma=False,
    )
```

profile of v0, /device:TPU:2, one launch (start us, length us, event | category | flops | bytes accessed | tf_op | source)
XLA Modules:
  0.0 525.7 jit_solution(14808827266614481248)
XLA Ops:
  7.2 0.0 copy-start
  7.2 0.0 copy-start.1
  7.2 0.9 convert_reduce_fusion
  8.1 0.1 copy.35
  8.2 0.7 convert_element_type.89
  8.9 1.3 fusion.8
  10.2 0.2 reduce_window_sum.11
  10.4 0.1 copy.37
  10.4 0.3 convolution_convert_fusion.2
  10.7 0.0 copy-done.1
  10.7 0.9 fusion.1
  11.7 71.8 %all_to_all.10 = bf16[32,1,16,2560]{3,2,1,0:T(8,128)(2,1)S(1)} all-to-all(bf16[32,1,16,2560]{3,2,1,0:T(8,128)(2,1)S(1)} %fusion.1), channel_id=1, replica_groups=mesh['gx'=32,'gy'=16] {'gx'}, dimensions={0} | all-to-all | bytes 5242880 | tf_op jit(solution)/shard_map/all_to_all | solution.py:74
  83.5 0.0 copy-done
  83.5 0.0 copy-start.5
  83.5 1.5 fusion.11
  85.0 0.0 copy-done.5
  85.0 2.4 fusion
  87.5 0.0 copy-start.6
  87.5 0.0 copy-start.2
  87.5 5.8 %all-to-all-start.1 = ((bf16[32,1,16,2560]{3,2,1,0:T(8,128)(2,1)}), bf16[32,1,16,2560]{3,2,1,0:T(8,128)(2,1)}, u32[]{:S(2)}, u32[]{:S(2)}) async-start(bf16[32,1,16,2560]{3,2,1,0:T(8,128)(2,1)} %fusion), calls=%async_computation.1 | async-start | bytes 5242880 | tf_op jit(solution)/shard_map/all_to_all | solution.py:82
  93.3 0.0 reduce-scatter.2.cloned.1.call-start
  93.3 0.0 copy-done.6
  93.3 0.4 fusion.26
  93.8 0.0 copy-done.2
  93.9 0.2 fusion.36
  94.1 0.0 copy-start.4
  94.1 58.5 %all-to-all-done.1 = bf16[32,1,16,2560]{3,2,1,0:T(8,128)(2,1)} async-done(((bf16[32,1,16,2560]{3,2,1,0:T(8,128)(2,1)}), bf16[32,1,16,2560]{3,2,1,0:T(8,128)(2,1)}, u32[]{:S(2)}, u32[]{:S(2)}) %all-to-all-start.1) | async-done | bytes 2621472 | tf_op jit(solution)/shard_map/all_to_all | solution.py:82
  152.6 4.5 convolution_bitcast_fusion
  157.1 0.0 copy-start.3
  157.1 0.0 reduce-scatter.2.cloned.1.call-update
  157.1 0.0 all-gather.3.cloned.1.call-start
  157.2 0.0 copy-done.4
  157.2 62.9 %reduce-scatter.2.cloned.1.call-done = f32[8,2560]{1,0:T(8,128)} async-done(((f32[128,2560]{1,0:T(8,128)}), f32[8,2560]{1,0:T(8,128)}) %reduce-scatter.2.cloned.1.call-update) | async-done | bytes 81936 | tf_op jit(solution)/shard_map/reduce_scatter | solution.py:86
  220.1 1.0 fusion.33
  221.1 0.7 fusion.35
  221.8 0.0 all-gather.3.cloned.1.call-update
  221.8 0.0 all-gather.5.cloned.1.call-start
  221.9 0.7 all-gather.5.cloned.1.call-update
  222.6 0.0 copy-done.3
  222.6 0.1 constant_dynamic-slice_fusion
  222.7 0.1 eq.70
  222.8 79.2 %all-gather.3.cloned.1.call-done = bf16[256,2560]{1,0:T(8,128)(2,1)} async-done(((bf16[8,2560]{1,0:T(8,128)(2,1)}), bf16[256,2560]{1,0:T(8,128)(2,1)}) %all-gather.3.cloned.1.call-update) | async-done | bytes 1310736 | tf_op jit(solution)/shard_map/all_gather | solution.py:90
  301.9 61.2 %all-gather.5.cloned.1.call-done = bf16[2560,1664]{1,0:T(8,128)(2,1)} async-done(((bf16[160,1664]{1,0:T(8,128)(2,1)}), bf16[2560,1664]{1,0:T(8,128)(2,1)}) %all-gather.5.cloned.1.call-update) | async-done | bytes 8519696 | tf_op jit(solution)/shard_map/all_gather | solution.py:94
  363.1 7.6 %fusion.45 = (f32[256]{0:T(256)S(1)}, f32[256,1664]{1,0:T(8,128)}) fusion(bf16[256,2560]{1,0:T(8,128)(2,1)} %all-gather.3.cloned.1.call-done, bf16[2560,1664]{1,0:T(8,128)(2,1)} %all-gather.5.cloned.1.call-done), kind=kOutput, calls=%fused_computation.68 | convolution fusion | flops 2181463808 | bytes 11535360 | tf_op jit(solution)/shard_map/dot_general | solution.py:92
  370.7 70.6 %pmax.7 = f32[256]{0:T(256)S(1)} all-reduce(f32[256]{0:T(256)S(1)} %get-tuple-element.18), channel_id=1, replica_groups=mesh['gx'=32,'gy'=16] {'gx'}, use_global_device_ids=true, to_apply=%region_12.13 | all-reduce | flops 256 | bytes 2048 | tf_op jit(solution)/shard_map/pmax | solution.py:102
  441.4 2.1 fusion.7
  443.5 74.1 %all-reduce = (f32[256]{0:T(256)S(1)}, f32[256]{0:T(256)S(1)}, f32[256]{0:T(256)S(1)}) all-reduce(f32[256]{0:T(256)S(1)} %get-tuple-element.10, f32[256]{0:T(256)S(1)} %get-tuple-element.9, f32[256]{0:T(256)S(1)} %get-tuple-element.8), channel_id=1, replica_groups=mesh['gx'=32,'gy'=16] {'gx'}, use_global_device_ids=true, to_apply=%region_10.11 | all-reduce | flops 768 | bytes 6144 | tf_op jit(solution)/shard_map/psum | solution.py:105
  517.6 0.1 reshape.187
  517.7 0.7 copy.42
  518.4 0.1 reshape.188
  518.5 0.7 copy.43
  (13 shorter events, 0.2 us)
Async XLA Ops:
  7.2 76.3 %copy-start = (bf16[1,2560,384]{2,1,0:T(8,128)(2,1)S(1)}, bf16[1,2560,384]{2,1,0:T(8,128)(2,1)}, u32[]{:S(2)}) copy-start(bf16[1,2560,384]{2,1,0:T(8,128)(2,1)} %param.13) | copy-start | bytes 5898244
  7.2 3.5 copy-start.1
  83.5 1.5 copy-start.5
  87.5 5.8 %copy-start.6 = (bf16[2560,64]{0,1:T(8,128)(2,1)S(1)}, bf16[2560,64]{0,1:T(8,128)(2,1)}, u32[]{:S(2)}) copy-start(bf16[2560,64]{0,1:T(8,128)(2,1)} %param.11) | copy-start | bytes 983044
  87.5 6.3 %copy-start.2 = (s32[128,6]{0,1:T(8,128)S(1)}, s32[128,6]{0,1:T(8,128)}, u32[]{:S(2)}) copy-start(s32[128,6]{0,1:T(8,128)} %param.12) | copy-start | bytes 9220
  87.5 65.1 %all-to-all-start.1 = ((bf16[32,1,16,2560]{3,2,1,0:T(8,128)(2,1)}), bf16[32,1,16,2560]{3,2,1,0:T(8,128)(2,1)}, u32[]{:S(2)}, u32[]{:S(2)}) async-start(bf16[32,1,16,2560]{3,2,1,0:T(8,128)(2,1)} %fusion), calls=%async_computation.1 | async-start | bytes 5242880 | tf_op jit(solution)/shard_map/all_to_all | solution.py:82
  93.3 126.8 %reduce-scatter.2.cloned.1.call-start = ((), (), s32[]{:S(2)}) async-start(), calls=%async_computation.3 | async-start | bytes 1392640 | tf_op jit(solution)/shard_map/reduce_scatter | solution.py:86
  94.1 63.1 %copy-start.4 = (bf16[2560]{0:T(1024)(128)(2,1)S(1)}, bf16[2560]{0:T(1024)(128)(2,1)}, u32[]{:S(2)}) copy-start(bf16[2560]{0:T(1024)(128)(2,1)} %param.15) | copy-start | bytes 15364
  157.1 65.5 %copy-start.3 = (s32[4096]{0:T(1024)S(1)}, s32[4096]{0:T(1024)}, u32[]{:S(2)}) copy-start(s32[4096]{0:T(1024)} %param.17) | copy-start | bytes 49156
  157.1 144.8 %all-gather.3.cloned.1.call-start = ((), (), s32[]{:S(2)}) async-start(), calls=%async_computation.4 | async-start | bytes 1351680 | tf_op jit(solution)/shard_map/all_gather | solution.py:90
  221.8 141.3 %all-gather.5.cloned.1.call-start = ((), (), s32[]{:S(2)}) async-start(), calls=%async_computation.5 | async-start | bytes 9052160 | tf_op jit(solution)/shard_map/all_gather | solution.py:94
Sparse Core Ops, SparseCore 0:
  157.2 62.7 reduce-scatter.1
  223.2 78.6 all-gather.2
  304.1 59.0 all-gather.4
where the time goes:
time: 526 us
  waiting for transfers between devices  262 us (50%)
  blocking collectives  217 us (41%)
  matrix products  17.9 us (3%)
  between operations  13.9 us (3%)
  other arithmetic  7.05 us (1%)
  starting transfers between devices  5.9 us (1%)
    all_gather x1, waiting for transfers between devices, shards(): gathered = lax.all_gather(final_states, 'gx', axis=0, tiled=True)  79.2 us
    psum x1, blocking collectives, shards(): lax.psum((jnp.sum(weights, -1), jnp.sum(weights * shifted, -1), jnp.sum(j...  74.1 us
    all_to_all x1, blocking collectives, shards(): lax.all_to_all(outgoing, 'gx', split_axis=0, concat_axis=0, tiled=True)  71.8 us
    pmax x1, blocking collectives, shards(): peak_value = lax.pmax(jnp.max(logits, -1), 'gx')  70.6 us
    reduce_scatter x1, waiting for transfers between devices, shards(): lax.psum_scatter(partial_value, 'gy', scatter_dimension=0, tiled=True)  62.9 us
    all_gather x1, waiting for transfers between devices, shards(): lax.all_gather(head_weight, 'gy', axis=0, tiled=True)  61.2 us
    all_to_all x1, waiting for transfers between devices, shards(): lax.all_to_all(result, 'gx', split_axis=0, concat_axis=0, tiled=True)  58.5 us
  transfers between devices with their start and end apart: 4, of which 4 were waited for; matrix products, arithmetic and copies ran while one was open for 0% of the time, Pallas kernels for 0%

commit v1 on v0

--- a/solution.py
+++ b/solution.py
@@ -87,7 +87,9 @@
     residual = lax.dynamic_slice_in_dim(hidden_in, lane_index * share_rows, share_rows, 0)
     layer_out = (residual.astype(jnp.float32) + summed).astype(jnp.bfloat16)
     final_states = rms_scale(layer_out, final_gain).astype(jnp.bfloat16)
-    gathered = lax.all_gather(final_states, "gx", axis=0, tiled=True)
+    gathered = jnp.concatenate(
+        lax.all_to_all(jnp.stack([final_states] * lax.axis_size("gx")), "gx", 0, 0), axis=0
+    )
     target_grid = targets.reshape(group_count, tok_rows)
     logits = jnp.dot(
         gathered,

time: 526 us -> 443 us (0.84)
  waiting for transfers between devices: 262 us -> 169 us
  starting transfers between devices: 5.9 us -> 15.8 us
    all_gather x1 -> x0, waiting for transfers between devices: 79.2 us -> none  [shards(): gathered = lax.all_gather(final_states, 'gx', axis=0, tiled=True)]
    all_gather x1, waiting for transfers between devices: 61.2 us -> 17.3 us  [shards(): lax.all_gather(head_weight, 'gy', axis=0, tiled=True)]
    all_to_all x0 -> x1, waiting for transfers between devices: none -> 30.2 us  [shards(): lax.all_to_all(jnp.stack([final_states] * lax.axis_size('gx')), 'gx', 0, 0)]
    all_to_all x0 -> x1, starting transfers between devices: none -> 9.93 us  [shards(): lax.all_to_all(jnp.stack([final_states] * lax.axis_size('gx')), 'gx', 0, 0)]
  transfers between devices with their start and end apart: 4 -> 4, of which waited for: 4 -> 4; matrix products, arithmetic and copies ran while one was open for 0% -> 1% of each run, Pallas kernels for 0% -> 0%
where the time goes in v1:
time: 443 us
  blocking collectives  217 us (49%)
  waiting for transfers between devices  169 us (38%)
  matrix products  17.9 us (4%)
  starting transfers between devices  15.8 us (4%)
  between operations  14.2 us (3%)
  other arithmetic  6.43 us (1%)
    psum x1, blocking collectives, shards(): lax.psum((jnp.sum(weights, -1), jnp.sum(weights * shifted, -1), jnp.sum(j...  74.1 us
    all_to_all x1, blocking collectives, shards(): lax.all_to_all(outgoing, 'gx', split_axis=0, concat_axis=0, tiled=True)  71.8 us
    pmax x1, blocking collectives, shards(): peak_value = lax.pmax(jnp.max(logits, -1), 'gx')  70.6 us
    reduce_scatter x1, waiting for transfers between devices, shards(): lax.psum_scatter(partial_value, 'gy', scatter_dimension=0, tiled=True)  62.2 us
    all_to_all x1, waiting for transfers between devices, shards(): lax.all_to_all(result, 'gx', split_axis=0, concat_axis=0, tiled=True)  58.5 us
    all_to_all x1, waiting for transfers between devices, shards(): lax.all_to_all(jnp.stack([final_states] * lax.axis_size('gx')), 'gx', 0, 0)  30.2 us
    all_gather x1, waiting for transfers between devices, shards(): lax.all_gather(head_weight, 'gy', axis=0, tiled=True)  17.3 us
    all_to_all x1, starting transfers between devices, shards(): lax.all_to_all(jnp.stack([final_states] * lax.axis_size('gx')), 'gx', 0, 0)  9.93 us
  transfers between devices with their start and end apart: 4, of which 4 were waited for; matrix products, arithmetic and copies ran while one was open for 1% of the time, Pallas kernels for 0%

profile of v1, /device:TPU:2, one launch (start us, length us, event | category | flops | bytes accessed | tf_op | source)
XLA Modules:
  0.0 442.9 jit_solution(2619498923444398972)
XLA Ops:
  7.2 0.0 copy-start
  7.2 0.0 copy-start.1
  7.2 0.9 convert_reduce_fusion
  8.1 0.1 copy.35
  8.2 0.7 convert_element_type.89
  8.9 1.3 fusion.8
  10.2 0.2 reduce_window_sum.11
  10.4 0.1 copy.37
  10.4 0.3 convolution_convert_fusion.2
  10.7 0.0 copy-done.1
  10.7 0.9 fusion.1
  11.7 71.8 %all_to_all.15 = bf16[32,1,16,2560]{3,2,1,0:T(8,128)(2,1)S(1)} all-to-all(bf16[32,1,16,2560]{3,2,1,0:T(8,128)(2,1)S(1)} %fusion.1), channel_id=1, replica_groups=mesh['gx'=32,'gy'=16] {'gx'}, dimensions={0} | all-to-all | bytes 5242880 | tf_op jit(solution)/shard_map/all_to_all | solution.py:74
  83.5 0.0 copy-done
  83.5 0.0 copy-start.5
  83.5 1.5 fusion.13
  85.0 0.0 copy-done.5
  85.0 2.4 fusion
  87.5 0.0 copy-start.6
  87.5 0.0 copy-start.2
  87.5 5.8 %all-to-all-start.1 = ((bf16[32,1,16,2560]{3,2,1,0:T(8,128)(2,1)}), bf16[32,1,16,2560]{3,2,1,0:T(8,128)(2,1)}, u32[]{:S(2)}, u32[]{:S(2)}) async-start(bf16[32,1,16,2560]{3,2,1,0:T(8,128)(2,1)} %fusion), calls=%async_computation.1 | async-start | bytes 5242880 | tf_op jit(solution)/shard_map/all_to_all | solution.py:82
  93.3 0.0 reduce-scatter.2.cloned.1.call-start
  93.3 0.0 copy-done.6
  93.3 0.4 fusion.28
  93.8 0.0 copy-done.2
  93.9 0.2 fusion.38
  94.1 58.5 %all-to-all-done.1 = bf16[32,1,16,2560]{3,2,1,0:T(8,128)(2,1)} async-done(((bf16[32,1,16,2560]{3,2,1,0:T(8,128)(2,1)}), bf16[32,1,16,2560]{3,2,1,0:T(8,128)(2,1)}, u32[]{:S(2)}, u32[]{:S(2)}) %all-to-all-start.1) | async-done | bytes 2621472 | tf_op jit(solution)/shard_map/all_to_all | solution.py:82
  152.6 4.6 %convolution_bitcast_fusion = f32[128,2560]{1,0:T(8,128)} fusion(bf16[32,1,16,2560]{3,2,1,0:T(8,128)(2,1)} %all-to-all-done.1, bf16[128,16,32]{0,2,1:T(8,128)(2,1)S(1)} %convolution_convert_fusion.2, f32[32,128]{1,0:T(8,128)S(1)} %fusion.38), kind=kOutput, calls=%fused_computation.4 | convolution fusion | flops 335740928 | bytes 4079616 | tf_op jit(solution)/shard_map/tkcn,tkcd->nd/dot_general | solution.py:83
  157.1 0.0 copy-start.4
  157.1 0.0 reduce-scatter.2.cloned.1.call-update
  157.2 0.0 all-gather.2.cloned.1.call-start
  157.2 0.7 all-gather.2.cloned.1.call-update
  157.9 0.0 copy-done.4
  157.9 62.2 %reduce-scatter.2.cloned.1.call-done = f32[8,2560]{1,0:T(8,128)} async-done(((f32[128,2560]{1,0:T(8,128)}), f32[8,2560]{1,0:T(8,128)}) %reduce-scatter.2.cloned.1.call-update) | async-done | bytes 81936 | tf_op jit(solution)/shard_map/reduce_scatter | solution.py:86
  220.1 1.0 fusion.35
  221.2 0.1 fusion.37
  221.2 0.0 copy-start.3
  221.3 1.2 stack.2
  222.5 9.9 %all-to-all-start.2 = ((bf16[32,8,2560]{2,1,0:T(8,128)(2,1)}), bf16[32,8,2560]{2,1,0:T(8,128)(2,1)}, u32[]{:S(2)}, u32[]{:S(2)}) async-start(bf16[32,8,2560]{2,1,0:T(8,128)(2,1)} %stack.2), calls=%async_computation.3 | async-start | bytes 2621440 | tf_op jit(solution)/shard_map/all_to_all | solution.py:91
  232.4 0.0 copy-done.3
  232.4 0.1 constant_dynamic-slice_fusion
  232.5 0.1 eq.70
  232.6 30.2 %all-to-all-done.2 = bf16[32,8,2560]{2,1,0:T(8,128)(2,1)} async-done(((bf16[32,8,2560]{2,1,0:T(8,128)(2,1)}), bf16[32,8,2560]{2,1,0:T(8,128)(2,1)}, u32[]{:S(2)}, u32[]{:S(2)}) %all-to-all-start.2) | async-done | bytes 1310752 | tf_op jit(solution)/shard_map/all_to_all | solution.py:91
  262.8 17.3 %all-gather.2.cloned.1.call-done = bf16[2560,1664]{1,0:T(8,128)(2,1)} async-done(((bf16[160,1664]{1,0:T(8,128)(2,1)}), bf16[2560,1664]{1,0:T(8,128)(2,1)}) %all-gather.2.cloned.1.call-update) | async-done | bytes 8519696 | tf_op jit(solution)/shard_map/all_gather | solution.py:96
  280.1 7.6 %fusion.47 = (f32[256]{0:T(256)S(1)}, f32[256,1664]{1,0:T(8,128)}) fusion(bf16[2560,1664]{1,0:T(8,128)(2,1)} %all-gather.2.cloned.1.call-done, bf16[32,8,2560]{2,1,0:T(8,128)(2,1)} %all-to-all-done.2), kind=kOutput, calls=%fused_computation.70 | convolution fusion | flops 2181463808 | bytes 11535360 | tf_op jit(solution)/shard_map/dot_general | solution.py:94
  287.7 70.6 %pmax.7 = f32[256]{0:T(256)S(1)} all-reduce(f32[256]{0:T(256)S(1)} %get-tuple-element.18), channel_id=1, replica_groups=mesh['gx'=32,'gy'=16] {'gx'}, use_global_device_ids=true, to_apply=%region_12.13 | all-reduce | flops 256 | bytes 2048 | tf_op jit(solution)/shard_map/pmax | solution.py:104
  358.3 2.1 fusion.7
  360.4 74.1 %all-reduce = (f32[256]{0:T(256)S(1)}, f32[256]{0:T(256)S(1)}, f32[256]{0:T(256)S(1)}) all-reduce(f32[256]{0:T(256)S(1)} %get-tuple-element.10, f32[256]{0:T(256)S(1)} %get-tuple-element.9, f32[256]{0:T(256)S(1)} %get-tuple-element.8), channel_id=1, replica_groups=mesh['gx'=32,'gy'=16] {'gx'}, use_global_device_ids=true, to_apply=%region_10.11 | all-reduce | flops 768 | bytes 6144 | tf_op jit(solution)/shard_map/psum | solution.py:107
  434.6 0.1 reshape.193
  434.7 0.7 copy.42
  435.3 0.1 reshape.194
  435.4 0.7 copy.43
  (13 shorter events, 0.2 us)
Async XLA Ops:
  7.2 76.3 %copy-start = (bf16[1,2560,384]{2,1,0:T(8,128)(2,1)S(1)}, bf16[1,2560,384]{2,1,0:T(8,128)(2,1)}, u32[]{:S(2)}) copy-start(bf16[1,2560,384]{2,1,0:T(8,128)(2,1)} %param.13) | copy-start | bytes 5898244
  7.2 3.5 copy-start.1
  83.5 1.5 copy-start.5
  87.5 5.8 %copy-start.6 = (bf16[2560,64]{0,1:T(8,128)(2,1)S(1)}, bf16[2560,64]{0,1:T(8,128)(2,1)}, u32[]{:S(2)}) copy-start(bf16[2560,64]{0,1:T(8,128)(2,1)} %param.11) | copy-start | bytes 983044
  87.5 6.3 %copy-start.2 = (s32[128,6]{0,1:T(8,128)S(1)}, s32[128,6]{0,1:T(8,128)}, u32[]{:S(2)}) copy-start(s32[128,6]{0,1:T(8,128)} %param.12) | copy-start | bytes 9220
  87.5 65.1 %all-to-all-start.1 = ((bf16[32,1,16,2560]{3,2,1,0:T(8,128)(2,1)}), bf16[32,1,16,2560]{3,2,1,0:T(8,128)(2,1)}, u32[]{:S(2)}, u32[]{:S(2)}) async-start(bf16[32,1,16,2560]{3,2,1,0:T(8,128)(2,1)} %fusion), calls=%async_computation.1 | async-start | bytes 5242880 | tf_op jit(solution)/shard_map/all_to_all | solution.py:82
  93.3 126.9 %reduce-scatter.2.cloned.1.call-start = ((), (), s32[]{:S(2)}) async-start(), calls=%async_computation.4 | async-start | bytes 1392640 | tf_op jit(solution)/shard_map/reduce_scatter | solution.py:86
  157.1 0.8 copy-start.4
  157.2 122.9 %all-gather.2.cloned.1.call-start = ((), (), s32[]{:S(2)}) async-start(), calls=%async_computation.5 | async-start | bytes 9052160 | tf_op jit(solution)/shard_map/all_gather | solution.py:96
  221.2 11.2 %copy-start.3 = (s32[4096]{0:T(1024)S(1)}, s32[4096]{0:T(1024)}, u32[]{:S(2)}) copy-start(s32[4096]{0:T(1024)} %param.17) | copy-start | bytes 49156
  222.5 40.3 %all-to-all-start.2 = ((bf16[32,8,2560]{2,1,0:T(8,128)(2,1)}), bf16[32,8,2560]{2,1,0:T(8,128)(2,1)}, u32[]{:S(2)}, u32[]{:S(2)}) async-start(bf16[32,8,2560]{2,1,0:T(8,128)(2,1)} %stack.2), calls=%async_computation.3 | async-start | bytes 2621440 | tf_op jit(solution)/shard_map/all_to_all | solution.py:91
Sparse Core Ops, SparseCore 0:
  157.3 62.7 reduce-scatter.1
  222.2 57.7 all-gather.1
